TPU v7x, 128 devices: a whole 4x4x4 slice. The times are simulated.
128 devices in a mesh: bin: 4 (over y), grp: 32 (over x, z, core).
Axes of the slice: x: 4, y: 4, z: 4, core: 2. Of those that a mesh axis runs over, the one named last changes fastest.
Arguments:
- templates: bfloat16 [131072, 512], P(('bin', 'grp')), may hold values from -6 to 6
- owner_device: int32 [131072, 1], P(('bin', 'grp')), may hold values from 0 to 127; in each aligned block of 1024 rows (0 to 1023, 1024 to 2047, ...) at most 16 rows name the same one
- rate_code: int32 [131072], P(('bin', 'grp')), may hold values from 0 to 4
- rate_gains: float32 [5, 512], replicated, may hold values from 0.5 to 2
- sketch: float32 [512, 256], replicated, may hold values from -6 to 6
- strain: float32 [2, 262144], P(None, 'grp'), may hold values from -6 to 6
Outputs:
- mixing: bfloat16 [131072, 256], P(('bin', 'grp'))
- spectrum: float32 [4, 256], P('bin')
- filtered_0: bfloat16 [4, 2, 262144, 256], P('bin', None, 'grp')
- filtered_1: bfloat16 [4, 2, 131072, 256], P('bin', None, 'grp')
- filtered_2: bfloat16 [4, 2, 65536, 256], P('bin', None, 'grp')
- filtered_3: bfloat16 [4, 2, 32768, 256], P('bin', None, 'grp')
- filtered_4: bfloat16 [4, 2, 16384, 256], P('bin', None, 'grp')
Inputs may be any that keep to these rules, and one draw needn't show every extreme that they name: `owner_device`: among the rows of one device, no device is named by more than 16 rows, and some device is named by exactly 16 rows.
All inputs are finite; a program needn't handle non-finite values.
Results may differ from a plain program's by a relative error of at most 0.0059.
Values may be sent and summed in bfloat16 or wider, within the bound.
A program may use at most 128 MiB of HBM per device.

v0:
```python
import math
import jax
import jax.numpy as jnp
from jax import lax
from jax.sharding import PartitionSpec as P

highest = lax.Precision.HIGHEST
inv_root_two = 0.7071067811865476


def shifted(x, axis, by):
    length = lax.axis_size(axis)
    pairs = [(i, i + by) for i in range(length) if 0 <= i + by < length]
    return lax.ppermute(x, axis, pairs)


def whiten_rows(templates, rate_code, rate_gains):
    factor = jnp.zeros(templates.shape, jnp.float32)
    for rate_level in range(rate_gains.shape[0]):
        factor = factor + jnp.where(
            (rate_code == rate_level)[:, None], rate_gains[rate_level][None, :], jnp.float32(0.0)
        )
    return (templates.astype(jnp.float32) * factor).astype(jnp.bfloat16)


def strain_levels(strain, count):
    current = strain
    level_list = []
    for rate_level in range(count):
        if rate_level > 0:
            paired = current.reshape(current.shape[0], -1, 2)
            current = (paired[:, :, 0] + paired[:, :, 1]) * inv_root_two
        level_list.append(current.astype(jnp.bfloat16))
    return level_list


def filter_level(history, rounded, basis_bf, stride):
    tap_rows = basis_bf[::stride]
    joined = jnp.concatenate([history[:, 1:], rounded], axis=1)
    return lax.conv_general_dilated(
        joined[:, :, None],
        tap_rows[::-1][:, None, :],
        (1,),
        "VALID",
        dimension_numbers=("NWC", "WIO", "NWC"),
        preferred_element_type=jnp.float32,
    )


def basis_from(product):
    inner_gram = jnp.dot(product.T, product, precision=highest)
    lower_factor = jnp.linalg.cholesky(inner_gram)
    basis_bf = jax.scipy.linalg.solve_triangular(lower_factor, product.T, lower=True).T.astype(
        jnp.bfloat16
    )
    return (basis_bf, jnp.diagonal(lower_factor))


def local(templates, owner_device, rate_code, rate_gains, sketch, strain):
    tpl_rows = templates.shape[0]
    slice_len = templates.shape[1]
    group_size = lax.axis_size("grp")
    bin_count = lax.axis_size("bin")
    devices = bin_count * group_size
    capacity = 2 * tpl_rows // devices
    scale_down = tpl_rows * group_size * math.sqrt(slice_len)
    whitened = whiten_rows(templates, rate_code, rate_gains)
    target = owner_device[:, 0]
    member_table = (target[:, None] == jnp.arange(devices, dtype=jnp.int32)[None, :]).astype(
        jnp.int32
    )
    rank_in_dest = jnp.sum(jnp.cumsum(member_table, axis=0) * member_table, axis=1) - 1
    slot_index = target * capacity + rank_in_dest
    outgoing = jnp.zeros((devices * capacity, slice_len), jnp.bfloat16).at[slot_index].set(whitened)
    received = lax.all_to_all(outgoing, ("bin", "grp"), split_axis=0, concat_axis=0, tiled=True)
    partial_gram = lax.dot_general(
        received, received, (((0,), (0,)), ((), ())), preferred_element_type=jnp.float32
    )
    gram_total = lax.psum(partial_gram, "grp")
    product = jnp.dot(gram_total, sketch, precision=highest)
    basis_bf, diag_here = basis_from(product)
    coeffs = jnp.dot(received, basis_bf, preferred_element_type=jnp.float32).astype(jnp.bfloat16)
    returned = lax.all_to_all(coeffs, ("bin", "grp"), split_axis=0, concat_axis=0, tiled=True)
    mixing = returned[slot_index]
    spectrum = (diag_here / scale_down)[None, :]
    levels = strain_levels(strain, rate_gains.shape[0])
    rim_list = [
        levels[rate_level][:, -(slice_len >> rate_level) :] for rate_level in range(len(levels))
    ]
    history = shifted((rim_list[0], rim_list[1], rim_list[2], rim_list[3], rim_list[4]), "grp", 1)
    filtered = []
    for rate_level in range(len(levels)):
        result_level = filter_level(
            history[rate_level], levels[rate_level], basis_bf, 2**rate_level
        )
        filtered.append(result_level.astype(jnp.bfloat16)[None])
    return (mixing, spectrum, filtered[0], filtered[1], filtered[2], filtered[3], filtered[4])


def solution(mesh):
    return jax.shard_map(
        local,
        mesh=mesh,
        in_specs=(
            P(("bin", "grp"), None),
            P(("bin", "grp"), None),
            P(("bin", "grp")),
            P(),
            P(),
            P(None, "grp"),
        ),
        out_specs=(
            P(("bin", "grp"), None),
            P("bin", None),
            P("bin", None, "grp", None),
            P("bin", None, "grp", None),
            P("bin", None, "grp", None),
            P("bin", None, "grp", None),
            P("bin", None, "grp", None),
        ),
        check_vma=False,
    )
```

profile of v0, /device:TPU:1, one launch (start us, length us, event | category | flops | bytes accessed | tf_op | source)
XLA Modules:
  0.0 488.1 jit_solution(5350892277837483940)
XLA Ops:
  9.0 7.3 %scatter_custom_fusion = bf16[2048,512]{1,0:T(8,128)(2,1)} fusion(s32[1024]{0:T(1024)S(1)} %bitcast.143, bf16[1024,512]{1,0:T(8,128)(2,1)S(1)} %copy-done.3, f32[512]{0:T(512)S(1)} %bitcast.149, f32[512]{0:T(512)S(1)} %bitcast.150, f32[512]{0:T(512)S(1)} %bitcast.147, f32[512]{0:T(512)S(1)} %bitcast.148, f32[]{:T(128)} %constant.105.clone.1, ...), kind=kCustom, calls=%fused_computation.26 | custom fusion | flops 6291456 | bytes 3161094 | tf_op jit(solution)/shard_map/scatter | solution.py:74
  16.3 12.0 %all-to-all-start = ((bf16[128,16,512]{2,1,0:T(8,128)(2,1)}), bf16[128,16,512]{2,1,0:T(8,128)(2,1)}, u32[]{:S(2)}, u32[]{:S(2)}) async-start(bf16[128,16,512]{2,1,0:T(8,128)(2,1)} %bitcast.12), calls=%async_computation | async-start | bytes 4194304 | tf_op jit(solution)/shard_map/all_to_all | solution.py:75
  28.4 3.7 collective-permute-start
  32.1 6.4 %reshape.114 = f32[2,4096,2]{2,1,0:T(8,128)} reshape(f32[2,8192]{1,0:T(2,128)S(1)} %copy-done.6) | data formatting | bytes 131072 | tf_op jit(solution)/shard_map/reshape | solution.py:31
  38.5 5.9 %convert_reduce_fusion = bf16[2,4096]{1,0:T(2,128)(2,1)S(1)} fusion(f32[2,4096,2]{2,1,0:T(8,128)} %reshape.114), kind=kLoop, calls=%fused_computation.17 | loop fusion | flops 24576 | bytes 81920 | tf_op jit(solution)/shard_map/convert_element_type | solution.py:33
  52.4 3.6 collective-permute-start.2
  71.7 4.5 convolution_bitcast_fusion
  78.0 104.7 %all-reduce.3.cloned.1.call-done = f32[512,512]{1,0:T(8,128)} async-done(((f32[512,512]{1,0:T(8,128)}), f32[512,512]{1,0:T(8,128)}) %all-reduce.3.cloned.1.call-update) | async-done | bytes 1048592 | tf_op jit(solution)/shard_map/psum | solution.py:79
  186.2 11.7 %cholesky.50 = f32[128,128]{1,0:T(8,128)S(1)} custom-call(f32[128,128]{1,0:T(8,128)S(1)} %cholesky.118), custom_call_target="Cholesky" | custom-call | tf_op jit(solution)/shard_map/jit(cholesky)/cholesky | solution.py:52
  197.9 9.8 %custom-call.15 = f32[1,128,128]{1,2,0:T(8,128)S(1)} custom-call(f32[1,128,128]{2,1,0:T(8,128)S(1)} %get-tuple-element.30), custom_call_target="InvertDiagBlocksLowerTriangular" | custom-call | tf_op jit(solution)/shard_map/jit(cholesky)/cholesky | solution.py:52
  208.2 12.2 %cholesky.105 = f32[128,128]{1,0:T(8,128)S(1)} custom-call(f32[128,128]{1,0:T(8,128)S(1)} %convolution_subtract_fusion.1), custom_call_target="Cholesky" | custom-call | tf_op jit(solution)/shard_map/jit(cholesky)/cholesky | solution.py:52
  222.5 4.0 while.1
  226.5 19.7 %custom-call.16 = f32[2,128,128]{1,2,0:T(8,128)S(1)} custom-call(f32[2,128,128]{2,1,0:T(8,128)S(1)} %get-tuple-element.14), custom_call_target="InvertDiagBlocksLowerTriangular" | custom-call | tf_op jit(solution)/shard_map/jit(_solve_triangular)/triangular_solve | solution.py:53
  248.5 6.6 %slice.147 = bf16[256,256]{0,1:T(8,128)(2,1)} slice(bf16[512,256]{0,1:T(8,128)(2,1)S(1)} %fusion.31), slice={[0:512:2], [0:256:1]} | slice | bytes 262144 | tf_op jit(solution)/shard_map/slice | solution.py:38
  261.3 3.3 convolution_convert_fusion
  264.6 8.5 %all-to-all-start.1 = ((bf16[128,16,256]{2,1,0:T(8,128)(2,1)}), bf16[128,16,256]{2,1,0:T(8,128)(2,1)}, u32[]{:S(2)}, u32[]{:S(2)}) async-start(bf16[128,16,256]{2,1,0:T(8,128)(2,1)} %bitcast.21), calls=%async_computation.1 | async-start | bytes 2097152 | tf_op jit(solution)/shard_map/all_to_all | solution.py:83
  276.4 123.6 %select_convert_fusion = bf16[16,1088,256]{2,0,1:T(8,128)(2,1)} fusion(pred[16,1088]{0,1:T(8,128)(4,1)S(1)} %bitcast.152, bf16[16,1599,1]{0,2,1:T(2,128)(2,1)S(1)} %copy.25, bf16[512,1,256]{2,1,0:T(2,128)(2,1)S(1)} %copy.26), kind=kOutput, calls=%fused_computation.5 | convolution fusion | flops 4572315648 | bytes 9243616 | tf_op jit(solution)/shard_map/conv_general_dilated | solution.py:40
  400.1 10.2 %copy.27 = bf16[16,1088,256]{2,1,0:T(8,128)(2,1)} copy(bf16[16,1088,256]{2,0,1:T(8,128)(2,1)} %select_convert_fusion) | data formatting | bytes 17825792 | tf_op jit(solution)/shard_map/convert_element_type | solution.py:96
  410.3 7.4 %slice_bitcast_fusion = bf16[1,2,8192,256]{3,2,1,0:T(8,128)(2,1)} fusion(bf16[2,8704,256]{2,1,0:T(8,128)(2,1)} %bitcast.129), kind=kLoop, calls=%fused_computation.7 | loop fusion | bytes 16777216 | tf_op jit(solution)/shard_map/broadcast_in_dim | solution.py:96
  418.3 31.3 %select_convert_fusion.1 = bf16[16,544,256]{2,0,1:T(8,128)(2,1)S(1)} fusion(pred[16,544]{0,1:T(8,128)(4,1)S(1)} %bitcast.153, bf16[16,799,1]{0,2,1:T(2,128)(2,1)S(1)} %copy-done.5, bf16[256,1,256]{2,1,0:T(2,128)(2,1)S(1)} %copy.29), kind=kOutput, calls=%fused_computation.6 | convolution fusion | flops 1145307136 | bytes 4621792 | tf_op jit(solution)/shard_map/conv_general_dilated | solution.py:40
  449.6 3.6 copy.30
  453.6 8.4 %select_convert_fusion.2 = bf16[16,272,256]{2,0,1:T(8,128)(2,1)S(1)} fusion(pred[16,272]{0,1:T(8,128)(4,1)S(1)} %copy-done.19, bf16[16,399,1]{0,2,1:T(2,128)(2,1)S(1)} %copy-done.10, bf16[128,1,256]{2,1,0:T(2,128)(2,1)S(1)} %copy.32), kind=kOutput, calls=%fused_computation.8 | convolution fusion | flops 287440896 | bytes 2310880 | tf_op jit(solution)/shard_map/conv_general_dilated | solution.py:40
  470.6 4.5 slice_bitcast_fusion.1
  475.0 6.0 %gather_fusion = bf16[1024,256]{1,0:T(8,128)(2,1)} fusion(bf16[2048,256]{1,0:T(8,128)(2,1)} %bitcast.22, s32[1024]{0:T(1024)S(1)} %copy-done.14), kind=kCustom, calls=%fused_computation | custom fusion | bytes 1052672 | tf_op jit(solution)/shard_map/gather | solution.py:84
  (169 shorter events, 57.0 us)
Async XLA Ops:
  7.2 175.5 %copy-start = (f32[512,256]{1,0:T(8,128)S(1)}, f32[512,256]{1,0:T(8,128)}, u32[]{:S(2)}) copy-start(f32[512,256]{1,0:T(8,128)} %param.10) | copy-start | bytes 1572868
  7.2 1.8 copy-start.16
  7.2 1.8 copy-start.3
  16.3 12.0 %copy-start.6 = (f32[2,8192]{1,0:T(2,128)S(1)}, f32[2,8192]{1,0:T(2,128)}, u32[]{:S(2)}) copy-start(f32[2,8192]{1,0:T(2,128)} %param.11) | copy-start | bytes 196612
  16.3 55.3 %all-to-all-start = ((bf16[128,16,512]{2,1,0:T(8,128)(2,1)}), bf16[128,16,512]{2,1,0:T(8,128)(2,1)}, u32[]{:S(2)}, u32[]{:S(2)}) async-start(bf16[128,16,512]{2,1,0:T(8,128)(2,1)} %bitcast.12), calls=%async_computation | async-start | bytes 4194304 | tf_op jit(solution)/shard_map/all_to_all | solution.py:75
  28.3 154.4 %all-reduce.3.cloned.1.call-start = ((), (), s32[]{:S(2)}) async-start(), calls=%async_computation.2 | async-start | bytes 2097152 | tf_op jit(solution)/shard_map/psum | solution.py:79
  28.4 43.2 %collective-permute-start = (bf16[2,512]{1,0:T(2,128)(2,1)S(1)}, bf16[2,512]{1,0:T(2,128)(2,1)S(1)}, u32[]{:S(2)}, u32[]{:S(2)}) collective-permute-start(bf16[2,512]{1,0:T(2,128)(2,1)S(1)} %slice.190), channel_id=1, source_target_pairs={{0,1},{1,2},{2,3},{3,4},{4,5},{5,6},{6,7},{7,8},{8,9},{9,10},{10,1... | collective-permute-start | bytes 6152 | tf_op jit(solution)/shard_map/ppermute | solution.py:14
  38.5 8.1 %copy-start.2 = (f32[2,4096,2]{2,1,0:T(8,128)S(1)}, f32[2,4096,2]{2,1,0:T(8,128)}, u32[]{:S(2)}) copy-start(f32[2,4096,2]{2,1,0:T(8,128)} %reshape.114) | copy-start | bytes 196612
  44.4 25.7 %collective-permute-start.1 = (bf16[2,256]{1,0:T(2,128)(2,1)S(1)}, bf16[2,256]{1,0:T(2,128)(2,1)S(1)}, u32[]{:S(2)}, u32[]{:S(2)}) collective-permute-start(bf16[2,256]{1,0:T(2,128)(2,1)S(1)} %slice.196), channel_id=1, source_target_pairs={{0,1},{1,2},{2,3},{3,4},{4,5},{5,6},{6,7},{7,8},{8,9},{9,10},{10,1... | collective-permute-start | bytes 3080 | tf_op jit(solution)/shard_map/ppermute | solution.py:14
  52.4 16.5 %collective-permute-start.2 = (bf16[2,128]{1,0:T(2,128)(2,1)S(1)}, bf16[2,128]{1,0:T(2,128)(2,1)S(1)}, u32[]{:S(2)}, u32[]{:S(2)}) collective-permute-start(bf16[2,128]{1,0:T(2,128)(2,1)S(1)} %slice.202), channel_id=1, source_target_pairs={{0,1},{1,2},{2,3},{3,4},{4,5},{5,6},{6,7},{7,8},{8,9},{9,10},{10,1... | collective-permute-start | bytes 1544 | tf_op jit(solution)/shard_map/ppermute | solution.py:14
  59.0 8.8 %collective-permute-start.3 = (bf16[2,64]{1,0:T(2,128)(2,1)S(1)}, bf16[2,64]{1,0:T(2,128)(2,1)S(1)}, u32[]{:S(2)}, u32[]{:S(2)}) collective-permute-start(bf16[2,64]{1,0:T(2,128)(2,1)S(1)} %slice.207), channel_id=1, source_target_pairs={{0,1},{1,2},{2,3},{3,4},{4,5},{5,6},{6,7},{7,8},{8,9},{9,10},{10,1... | collective-permute-start | bytes 776 | tf_op jit(solution)/shard_map/ppermute | solution.py:14
  62.7 4.0 collective-permute-start.4
  264.6 11.8 %copy-start.17 = (pred[16,1088]{0,1:T(32,128)(4,1)S(1)}, pred[16,1088]{0,1:T(32,128)(4,1)}, u32[]{:S(2)}) copy-start(pred[16,1088]{0,1:T(32,128)(4,1)} %constant.152) | copy-start | bytes 52228
  264.6 210.4 %all-to-all-start.1 = ((bf16[128,16,256]{2,1,0:T(8,128)(2,1)}), bf16[128,16,256]{2,1,0:T(8,128)(2,1)}, u32[]{:S(2)}, u32[]{:S(2)}) async-start(bf16[128,16,256]{2,1,0:T(8,128)(2,1)} %bitcast.21), calls=%async_computation.1 | async-start | bytes 2097152 | tf_op jit(solution)/shard_map/all_to_all | solution.py:83
  410.3 7.4 %copy-start.4 = (bf16[256,256]{0,1:T(8,128)(2,1)S(1)}, bf16[256,256]{0,1:T(8,128)(2,1)}, u32[]{:S(2)}) copy-start(bf16[256,256]{0,1:T(8,128)(2,1)} %slice.147) | copy-start | bytes 393220
  410.3 8.0 %copy-start.5 = (bf16[16,799,1]{0,2,1:T(2,128)(2,1)S(1)}, bf16[16,799,1]{0,2,1:T(2,128)(2,1)}, u32[]{:S(2)}) copy-start(bf16[16,799,1]{0,2,1:T(2,128)(2,1)} %copy.28) | copy-start | bytes 76708
  410.3 8.0 %copy-start.18 = (pred[16,544]{0,1:T(32,128)(4,1)S(1)}, pred[16,544]{0,1:T(32,128)(4,1)}, u32[]{:S(2)}) copy-start(pred[16,544]{0,1:T(32,128)(4,1)} %constant.153) | copy-start | bytes 26116
  449.6 3.7 copy-start.9
  449.6 4.0 copy-start.10
  449.6 4.0 copy-start.19
  462.7 1.8 copy-start.11
  462.8 1.8 copy-start.20
  470.6 4.5 copy-start.14
  475.0 6.0 %copy-start.1 = (f32[512,256]{1,0:T(8,128)S(1)}, f32[512,256]{1,0:T(8,128)}, u32[]{:S(2)}) copy-start(f32[512,256]{1,0:T(8,128)} %param.10) | copy-start | bytes 1572868
  (6 other events, 9.5 us)
Sparse Core Ops, SparseCore 0:
  76.3 106.3 all-reduce.2
where the time goes:
time: 496 us; the launch traced here: 488 us
  matrix products  179 us (36%)
  waiting for transfers between devices  105 us (21%)
  other arithmetic  76.5 us (15%)
  local copies, waits for them, and re-layouts  75.8 us (15%)
  starting transfers between devices  35.3 us (7%)
  between operations  16.3 us (3%)
    conv_general_dilated x5, matrix products, filter_level(): lax.conv_general_dilated(joined[:, :, None], tap_rows[::-1][:, None, :],...  166 us
    psum x1, waiting for transfers between devices, local(): gram_total = lax.psum(partial_gram, 'grp')  105 us
    another operation x6, other arithmetic, basis_from(): lower_factor = jnp.linalg.cholesky(inner_gram)  34.4 us
    another operation x3, other arithmetic, basis_from(): jax.scipy.linalg.solve_triangular(lower_factor, product.T, lower=True)  19.7 us
    convert_element_type x6, local copies, waits for them, and re-layouts, local(): filtered.append(result_level.astype(jnp.bfloat16)[None])  15.2 us
    broadcast_in_dim x5, local copies, waits for them, and re-layouts, local(): filtered.append(result_level.astype(jnp.bfloat16)[None])  15.2 us
    ppermute x5, starting transfers between devices, shifted(): return lax.ppermute(x, axis, pairs)  14.9 us
    slice x4, local copies, waits for them, and re-layouts, filter_level(): tap_rows = basis_bf[::stride]  12.8 us
  transfers between devices with their start and end apart: 8, of which 2 were waited for; matrix products, arithmetic and copies ran while one was open for 47% of the time, Pallas kernels for 0%

commit v1 on v0

--- a/solution.py
+++ b/solution.py
@@ -76,7 +76,11 @@
     partial_gram = lax.dot_general(
         received, received, (((0,), (0,)), ((), ())), preferred_element_type=jnp.float32
     )
-    gram_total = lax.psum(partial_gram, "grp")
+    gram_total = partial_gram
+    for hop in (1, 2, 4, 8, 16):
+        gram_total = gram_total + lax.ppermute(
+            gram_total, "grp", [(dev, dev ^ hop) for dev in range(32)]
+        )
     product = jnp.dot(gram_total, sketch, precision=highest)
     basis_bf, diag_here = basis_from(product)
     coeffs = jnp.dot(received, basis_bf, preferred_element_type=jnp.float32).astype(jnp.bfloat16)

time: 496 us -> 480 us (0.968)
  blocking collectives: 0 us -> 41.5 us
  waiting for transfers between devices: 105 us -> 66.8 us
  between operations: 16.3 us -> 2.93 us
  starting transfers between devices: 35.3 us -> 27.9 us
  other arithmetic: 76.5 us -> 82 us
  matrix products: 179 us -> 174 us
    psum x1 -> x0, waiting for transfers between devices: 105 us -> none  [local(): gram_total = lax.psum(partial_gram, 'grp')]
    ppermute x0 -> x5, waiting for transfers between devices: none -> 50.8 us  [local(): lax.ppermute(gram_total, 'grp', [(dev, dev ^ hop) for dev in range(32)])]
    all_to_all x0 -> x1, blocking collectives: none -> 41.5 us  [local(): lax.all_to_all(outgoing, ('bin', 'grp'), split_axis=0, concat_axis=0, til...]
    ppermute x5, waiting for transfers between devices: 0.1 us -> 16 us  [shifted(): return lax.ppermute(x, axis, pairs)]
    all_to_all x1 -> x0, starting transfers between devices: 12 us -> none  [local(): lax.all_to_all(outgoing, ('bin', 'grp'), split_axis=0, concat_axis=0, til...]
    ppermute x0 -> x5, starting transfers between devices: none -> 6.32 us  [local(): lax.ppermute(gram_total, 'grp', [(dev, dev ^ hop) for dev in range(32)])]
    add x0 -> x4, other arithmetic: none -> 5.86 us  [local(): gram_total + lax.ppermute(gram_total, 'grp', [(dev, dev ^ hop) for dev in...]
  transfers between devices with their start and end apart: 8 -> 11, of which waited for: 2 -> 4; matrix products, arithmetic and copies ran while one was open for 47% -> 50% of each run, Pallas kernels for 0% -> 0%
where the time goes in v1:
time: 480 us; the launch traced here: 471 us
  matrix products  174 us (36%)
  other arithmetic  82 us (17%)
  local copies, waits for them, and re-layouts  76.4 us (16%)
  waiting for transfers between devices  66.8 us (14%)
  blocking collectives  41.5 us (9%)
  starting transfers between devices  27.9 us (6%)
    conv_general_dilated x5, matrix products, filter_level(): lax.conv_general_dilated(joined[:, :, None], tap_rows[::-1][:, None, :],...  166 us
    ppermute x5, waiting for transfers between devices, local(): lax.ppermute(gram_total, 'grp', [(dev, dev ^ hop) for dev in range(32)])  50.8 us
    all_to_all x1, blocking collectives, local(): lax.all_to_all(outgoing, ('bin', 'grp'), split_axis=0, concat_axis=0, til...  41.5 us
    another operation x6, other arithmetic, basis_from(): lower_factor = jnp.linalg.cholesky(inner_gram)  34.4 us
    another operation x3, other arithmetic, basis_from(): jax.scipy.linalg.solve_triangular(lower_factor, product.T, lower=True)  19.7 us
    ppermute x5, waiting for transfers between devices, shifted(): return lax.ppermute(x, axis, pairs)  16 us
    convert_element_type x6, local copies, waits for them, and re-layouts, local(): filtered.append(result_level.astype(jnp.bfloat16)[None])  15.2 us
    broadcast_in_dim x5, local copies, waits for them, and re-layouts, local(): filtered.append(result_level.astype(jnp.bfloat16)[None])  15.2 us
  transfers between devices with their start and end apart: 11, of which 4 were waited for; matrix products, arithmetic and copies ran while one was open for 50% of the time, Pallas kernels for 0%

profile of v1, /device:TPU:1, one launch (start us, length us, event | category | flops | bytes accessed | tf_op | source)
XLA Modules:
  0.0 471.4 jit_solution(12604310133420333948)
XLA Ops:
  2.4 6.9 %scatter_custom_fusion = bf16[2048,512]{1,0:T(8,128)(2,1)S(1)} fusion(s32[1024]{0:T(1024)S(1)} %bitcast.144, bf16[1024,512]{1,0:T(8,128)(2,1)} %param.6, f32[512]{0:T(512)S(1)} %bitcast.150, f32[512]{0:T(512)S(1)} %bitcast.151, f32[512]{0:T(512)S(1)} %bitcast.148, f32[512]{0:T(512)S(1)} %bitcast.149, f32[]{:T(128)} %constant.105.clone.1, ...), kind=kCustom, calls=%fused_computation.25 | custom fusion | flops 6291456 | bytes 3161094 | tf_op jit(solution)/shard_map/scatter | solution.py:74
  9.3 41.5 %all_to_all.24 = bf16[128,16,512]{2,1,0:T(8,128)(2,1)S(1)} all-to-all(bf16[128,16,512]{2,1,0:T(8,128)(2,1)S(1)} %bitcast.131), channel_id=1, replica_groups=mesh['bin'=4,'grp'=32] {'bin','grp'}, dimensions={0} | all-to-all | bytes 4194304 | tf_op jit(solution)/shard_map/all_to_all | solution.py:75
  55.5 6.4 %reshape.114 = f32[2,4096,2]{2,1,0:T(8,128)} reshape(f32[2,8192]{1,0:T(2,128)S(1)} %copy-done.8) | data formatting | bytes 131072 | tf_op jit(solution)/shard_map/reshape | solution.py:31
  61.9 5.9 %convert_reduce_fusion = bf16[2,4096]{1,0:T(2,128)(2,1)S(1)} fusion(f32[2,4096,2]{2,1,0:T(8,128)} %reshape.114), kind=kLoop, calls=%fused_computation.17 | loop fusion | flops 24576 | bytes 81920 | tf_op jit(solution)/shard_map/convert_element_type | solution.py:33
  77.2 3.7 collective-permute-start.7
  86.8 9.6 %collective-permute-done.1 = f32[512,512]{1,0:T(8,128)} collective-permute-done((f32[512,512]{1,0:T(8,128)}, f32[512,512]{1,0:T(8,128)}, u32[]{:S(2)}, u32[]{:S(2)}) %collective-permute-start.1) | collective-permute-done | bytes 1048608 | tf_op jit(solution)/shard_map/ppermute | solution.py:81
  107.1 16.0 %collective-permute-done.8 = bf16[2,64]{1,0:T(2,128)(2,1)S(1)} collective-permute-done((bf16[2,64]{1,0:T(2,128)(2,1)S(1)}, bf16[2,64]{1,0:T(2,128)(2,1)S(1)}, u32[]{:S(2)}, u32[]{:S(2)}) %collective-permute-start.8) | collective-permute-done | bytes 288 | tf_op jit(solution)/shard_map/ppermute | solution.py:14
  128.6 21.0 %collective-permute-done.3 = f32[512,512]{1,0:T(8,128)} collective-permute-done((f32[512,512]{1,0:T(8,128)S(1)}, f32[512,512]{1,0:T(8,128)}, u32[]{:S(2)}, u32[]{:S(2)}) %collective-permute-start.3) | collective-permute-done | bytes 1048608 | tf_op jit(solution)/shard_map/ppermute | solution.py:81
  155.2 20.2 %collective-permute-done.4 = f32[512,512]{1,0:T(8,128)} collective-permute-done((f32[512,512]{1,0:T(8,128)S(1)}, f32[512,512]{1,0:T(8,128)}, u32[]{:S(2)}, u32[]{:S(2)}) %collective-permute-start.4) | collective-permute-done | bytes 1048608 | tf_op jit(solution)/shard_map/ppermute | solution.py:81
  178.9 11.7 %cholesky.50 = f32[128,128]{1,0:T(8,128)S(1)} custom-call(f32[128,128]{1,0:T(8,128)S(1)} %cholesky.118), custom_call_target="Cholesky" | custom-call | tf_op jit(solution)/shard_map/jit(cholesky)/cholesky | solution.py:52
  190.7 9.8 %custom-call.15 = f32[1,128,128]{1,2,0:T(8,128)S(1)} custom-call(f32[1,128,128]{2,1,0:T(8,128)S(1)} %get-tuple-element.30), custom_call_target="InvertDiagBlocksLowerTriangular" | custom-call | tf_op jit(solution)/shard_map/jit(cholesky)/cholesky | solution.py:52
  201.0 12.2 %cholesky.105 = f32[128,128]{1,0:T(8,128)S(1)} custom-call(f32[128,128]{1,0:T(8,128)S(1)} %convolution_subtract_fusion), custom_call_target="Cholesky" | custom-call | tf_op jit(solution)/shard_map/jit(cholesky)/cholesky | solution.py:52
  215.2 4.0 while.1
  219.2 19.7 %custom-call.16 = f32[2,128,128]{1,2,0:T(8,128)S(1)} custom-call(f32[2,128,128]{2,1,0:T(8,128)S(1)} %get-tuple-element.14), custom_call_target="InvertDiagBlocksLowerTriangular" | custom-call | tf_op jit(solution)/shard_map/jit(_solve_triangular)/triangular_solve | solution.py:53
  241.3 6.6 %slice.147 = bf16[256,256]{0,1:T(8,128)(2,1)} slice(bf16[512,256]{0,1:T(8,128)(2,1)S(1)} %fusion.33), slice={[0:512:2], [0:256:1]} | slice | bytes 262144 | tf_op jit(solution)/shard_map/slice | solution.py:38
  255.8 8.2 %all-to-all-start.1 = ((bf16[128,16,256]{2,1,0:T(8,128)(2,1)}), bf16[128,16,256]{2,1,0:T(8,128)(2,1)}, u32[]{:S(2)}, u32[]{:S(2)}) async-start(bf16[128,16,256]{2,1,0:T(8,128)(2,1)} %bitcast.137), calls=%async_computation.1 | async-start | bytes 2097152 | tf_op jit(solution)/shard_map/all_to_all | solution.py:87
  267.3 123.0 %select_convert_fusion = bf16[16,1088,256]{2,0,1:T(8,128)(2,1)} fusion(pred[16,1088]{0,1:T(8,128)(4,1)S(1)} %bitcast.153, bf16[16,1599,1]{0,2,1:T(2,128)(2,1)S(1)} %copy-done.5, bf16[512,1,256]{2,1,0:T(2,128)(2,1)S(1)} %copy.51), kind=kOutput, calls=%fused_computation.5 | convolution fusion | flops 4572315648 | bytes 9243616 | tf_op jit(solution)/shard_map/conv_general_dilated | solution.py:40
  390.3 10.2 %copy.52 = bf16[16,1088,256]{2,1,0:T(8,128)(2,1)} copy(bf16[16,1088,256]{2,0,1:T(8,128)(2,1)} %select_convert_fusion) | data formatting | bytes 17825792 | tf_op jit(solution)/shard_map/convert_element_type | solution.py:100
  400.5 7.4 %slice_bitcast_fusion = bf16[1,2,8192,256]{3,2,1,0:T(8,128)(2,1)} fusion(bf16[2,8704,256]{2,1,0:T(8,128)(2,1)} %bitcast.127), kind=kLoop, calls=%fused_computation.7 | loop fusion | bytes 16777216 | tf_op jit(solution)/shard_map/broadcast_in_dim | solution.py:100
  408.5 31.3 %select_convert_fusion.1 = bf16[16,544,256]{2,0,1:T(8,128)(2,1)S(1)} fusion(pred[16,544]{0,1:T(8,128)(4,1)S(1)} %bitcast.154, bf16[16,799,1]{0,2,1:T(2,128)(2,1)S(1)} %copy-done.7, bf16[256,1,256]{2,1,0:T(2,128)(2,1)S(1)} %copy.54), kind=kOutput, calls=%fused_computation.6 | convolution fusion | flops 1145307136 | bytes 4621792 | tf_op jit(solution)/shard_map/conv_general_dilated | solution.py:40
  439.8 3.6 copy.55
  443.8 8.4 %select_convert_fusion.2 = bf16[16,272,256]{2,0,1:T(8,128)(2,1)S(1)} fusion(pred[16,272]{0,1:T(8,128)(4,1)S(1)} %copy-done.21, bf16[16,399,1]{0,2,1:T(2,128)(2,1)S(1)} %copy-done.12, bf16[128,1,256]{2,1,0:T(2,128)(2,1)S(1)} %copy.57), kind=kOutput, calls=%fused_computation.8 | convolution fusion | flops 287440896 | bytes 2310880 | tf_op jit(solution)/shard_map/conv_general_dilated | solution.py:40
  460.7 4.5 slice_bitcast_fusion.1
  465.2 6.0 %gather_fusion = bf16[1024,256]{1,0:T(8,128)(2,1)} fusion(bf16[2048,256]{1,0:T(8,128)(2,1)} %bitcast.22, s32[1024]{0:T(1024)S(1)} %copy-done.16), kind=kCustom, calls=%fused_computation | custom fusion | bytes 1052672 | tf_op jit(solution)/shard_map/gather | solution.py:88
  (183 shorter events, 74.9 us)
Async XLA Ops:
  0.6 174.7 %copy-start = (f32[512,256]{1,0:T(8,128)S(1)}, f32[512,256]{1,0:T(8,128)}, u32[]{:S(2)}) copy-start(f32[512,256]{1,0:T(8,128)} %param.10) | copy-start | bytes 1572868
  52.2 17.9 %collective-permute-start = (f32[512,512]{1,0:T(8,128)S(1)}, f32[512,512]{1,0:T(8,128)S(1)}, u32[]{:S(2)}, u32[]{:S(2)}) collective-permute-start(f32[512,512]{1,0:T(8,128)S(1)} %convolution_bitcast_fusion), channel_id=1, source_target_pairs={{0,1},{1,0},{2,3},{3,2},{4,5},{5,4},{6,7},{7,6},{8,9},{9,8},{10,11... | collective-permute-start | bytes 3145736 | tf_op jit(solution)/shard_map/ppermute | solution.py:81
  53.6 74.9 %collective-permute-start.5 = (bf16[2,512]{1,0:T(2,128)(2,1)S(1)}, bf16[2,512]{1,0:T(2,128)(2,1)S(1)}, u32[]{:S(2)}, u32[]{:S(2)}) collective-permute-start(bf16[2,512]{1,0:T(2,128)(2,1)S(1)} %slice.190), channel_id=1, source_target_pairs={{0,1},{1,2},{2,3},{3,4},{4,5},{5,6},{6,7},{7,8},{8,9},{9,10},{10,1... | collective-permute-start | bytes 6152 | tf_op jit(solution)/shard_map/ppermute | solution.py:14
  61.9 9.5 %copy-start.2 = (f32[2,4096,2]{2,1,0:T(8,128)S(1)}, f32[2,4096,2]{2,1,0:T(8,128)}, u32[]{:S(2)}) copy-start(f32[2,4096,2]{2,1,0:T(8,128)} %reshape.114) | copy-start | bytes 196612
  67.8 59.2 %collective-permute-start.6 = (bf16[2,256]{1,0:T(2,128)(2,1)S(1)}, bf16[2,256]{1,0:T(2,128)(2,1)S(1)}, u32[]{:S(2)}, u32[]{:S(2)}) collective-permute-start(bf16[2,256]{1,0:T(2,128)(2,1)S(1)} %slice.196), channel_id=1, source_target_pairs={{0,1},{1,2},{2,3},{3,4},{4,5},{5,6},{6,7},{7,8},{8,9},{9,10},{10,1... | collective-permute-start | bytes 3080 | tf_op jit(solution)/shard_map/ppermute | solution.py:14
  71.3 25.1 %collective-permute-start.1 = (f32[512,512]{1,0:T(8,128)}, f32[512,512]{1,0:T(8,128)}, u32[]{:S(2)}, u32[]{:S(2)}) collective-permute-start(f32[512,512]{1,0:T(8,128)} %add.100), channel_id=1, source_target_pairs={{0,2},{1,3},{2,0},{3,1},{4,6},{5,7},{6,4},{7,5},{8,10},{9,11},{10,... | collective-permute-start | bytes 3145736 | tf_op jit(solution)/shard_map/ppermute | solution.py:81
  77.2 47.0 %collective-permute-start.7 = (bf16[2,128]{1,0:T(2,128)(2,1)S(1)}, bf16[2,128]{1,0:T(2,128)(2,1)S(1)}, u32[]{:S(2)}, u32[]{:S(2)}) collective-permute-start(bf16[2,128]{1,0:T(2,128)(2,1)S(1)} %slice.202), channel_id=1, source_target_pairs={{0,1},{1,2},{2,3},{3,4},{4,5},{5,6},{6,7},{7,8},{8,9},{9,10},{10,1... | collective-permute-start | bytes 1544 | tf_op jit(solution)/shard_map/ppermute | solution.py:14
  84.8 17.7 %collective-permute-start.9 = (bf16[2,32]{1,0:T(2,128)(2,1)S(1)}, bf16[2,32]{1,0:T(2,128)(2,1)S(1)}, u32[]{:S(2)}, u32[]{:S(2)}) collective-permute-start(bf16[2,32]{1,0:T(2,128)(2,1)S(1)} %slice.212), channel_id=1, source_target_pairs={{0,1},{1,2},{2,3},{3,4},{4,5},{5,6},{6,7},{7,8},{8,9},{9,10},{10,1... | collective-permute-start | bytes 392 | tf_op jit(solution)/shard_map/ppermute | solution.py:14
  98.1 26.2 %collective-permute-start.2 = (f32[512,512]{1,0:T(8,128)S(1)}, f32[512,512]{1,0:T(8,128)}, u32[]{:S(2)}, u32[]{:S(2)}) collective-permute-start(f32[512,512]{1,0:T(8,128)S(1)} %add.101), channel_id=1, source_target_pairs={{0,4},{1,5},{2,6},{3,7},{4,0},{5,1},{6,2},{7,3},{8,12},{9,13},{10,... | collective-permute-start | bytes 3145736 | tf_op jit(solution)/shard_map/ppermute | solution.py:81
  102.5 20.6 %collective-permute-start.8 = (bf16[2,64]{1,0:T(2,128)(2,1)S(1)}, bf16[2,64]{1,0:T(2,128)(2,1)S(1)}, u32[]{:S(2)}, u32[]{:S(2)}) collective-permute-start(bf16[2,64]{1,0:T(2,128)(2,1)S(1)} %slice.207), channel_id=1, source_target_pairs={{0,1},{1,2},{2,3},{3,4},{4,5},{5,6},{6,7},{7,8},{8,9},{9,10},{10,1... | collective-permute-start | bytes 776 | tf_op jit(solution)/shard_map/ppermute | solution.py:14
  125.8 23.8 %collective-permute-start.3 = (f32[512,512]{1,0:T(8,128)S(1)}, f32[512,512]{1,0:T(8,128)}, u32[]{:S(2)}, u32[]{:S(2)}) collective-permute-start(f32[512,512]{1,0:T(8,128)S(1)} %add.102), channel_id=1, source_target_pairs={{0,8},{1,9},{2,10},{3,11},{4,12},{5,13},{6,14},{7,15},{8,0},{9,1},... | collective-permute-start | bytes 3145736 | tf_op jit(solution)/shard_map/ppermute | solution.py:81
  151.0 24.3 %collective-permute-start.4 = (f32[512,512]{1,0:T(8,128)S(1)}, f32[512,512]{1,0:T(8,128)}, u32[]{:S(2)}, u32[]{:S(2)}) collective-permute-start(f32[512,512]{1,0:T(8,128)S(1)} %add.103), channel_id=1, source_target_pairs={{0,16},{1,17},{2,18},{3,19},{4,20},{5,21},{6,22},{7,23},{8,24},{9,... | collective-permute-start | bytes 3145736 | tf_op jit(solution)/shard_map/ppermute | solution.py:81
  215.2 38.8 %copy-start.4 = (bf16[128,16,512]{2,1,0:T(8,128)(2,1)S(1)}, bf16[128,16,512]{2,1,0:T(8,128)(2,1)}, u32[]{:S(2)}) copy-start(bf16[128,16,512]{2,1,0:T(8,128)(2,1)} %copy-done.3) | copy-start | bytes 6291460
  255.8 11.5 %copy-start.5 = (bf16[16,1599,1]{0,2,1:T(2,128)(2,1)S(1)}, bf16[16,1599,1]{0,2,1:T(2,128)(2,1)}, u32[]{:S(2)}) copy-start(bf16[16,1599,1]{0,2,1:T(2,128)(2,1)} %copy.50) | copy-start | bytes 153508
  255.8 11.5 %copy-start.19 = (pred[16,1088]{0,1:T(32,128)(4,1)S(1)}, pred[16,1088]{0,1:T(32,128)(4,1)}, u32[]{:S(2)}) copy-start(pred[16,1088]{0,1:T(32,128)(4,1)} %constant.152) | copy-start | bytes 52228
  255.8 209.4 %all-to-all-start.1 = ((bf16[128,16,256]{2,1,0:T(8,128)(2,1)}), bf16[128,16,256]{2,1,0:T(8,128)(2,1)}, u32[]{:S(2)}, u32[]{:S(2)}) async-start(bf16[128,16,256]{2,1,0:T(8,128)(2,1)} %bitcast.137), calls=%async_computation.1 | async-start | bytes 2097152 | tf_op jit(solution)/shard_map/all_to_all | solution.py:87
  400.5 7.4 %copy-start.6 = (bf16[256,256]{0,1:T(8,128)(2,1)S(1)}, bf16[256,256]{0,1:T(8,128)(2,1)}, u32[]{:S(2)}) copy-start(bf16[256,256]{0,1:T(8,128)(2,1)} %slice.147) | copy-start | bytes 393220
  400.5 8.0 %copy-start.7 = (bf16[16,799,1]{0,2,1:T(2,128)(2,1)S(1)}, bf16[16,799,1]{0,2,1:T(2,128)(2,1)}, u32[]{:S(2)}) copy-start(bf16[16,799,1]{0,2,1:T(2,128)(2,1)} %copy.53) | copy-start | bytes 76708
  400.5 8.0 %copy-start.20 = (pred[16,544]{0,1:T(32,128)(4,1)S(1)}, pred[16,544]{0,1:T(32,128)(4,1)}, u32[]{:S(2)}) copy-start(pred[16,544]{0,1:T(32,128)(4,1)} %constant.153) | copy-start | bytes 26116
  439.8 3.7 copy-start.11
  439.8 4.0 copy-start.12
  439.8 4.0 copy-start.21
  460.7 4.5 copy-start.16
  465.2 6.0 %copy-start.1 = (f32[512,256]{1,0:T(8,128)S(1)}, f32[512,256]{1,0:T(8,128)}, u32[]{:S(2)}) copy-start(f32[512,256]{1,0:T(8,128)} %param.10) | copy-start | bytes 1572868
  (11 other events, 18.6 us)
